TPU v7x, 32 devices: a whole 2x2x4 slice. The times are simulated.
32 devices in a mesh: dp: 4 (over y, core), fsdp: 8 (over z, x).
Axes of the slice: x: 2, y: 2, z: 4, core: 2. Of those that a mesh axis runs over, the one named last changes fastest.
Arguments:
- hidden_in: bfloat16 [20480, 768], P(('dp', 'fsdp')), may hold values from -7 to 7
- prev_logits: bfloat16 [32, 12, 640, 640], P(('dp', 'fsdp')), may hold values from -6 to 6
- segment_ids: int32 [32, 640], P(('dp', 'fsdp')), may hold values from 0 to 3, never falling along the last dimension, each value on 1 to 320 neighbouring positions
- d_hidden: bfloat16 [20480, 768], P(('dp', 'fsdp')), may hold values from -6 to 6
- d_logits: bfloat16 [32, 12, 640, 640], P(('dp', 'fsdp')), may hold values from -3 to 3
- weight_in: float32 [768, 5376], P(('dp', 'fsdp')), may hold values from -2.5 to 2.5
- weight_out: float32 [3840, 768], P(('dp', 'fsdp')), may hold values from -2 to 2
- vectors: float32 [12, 768], P(None, ('dp', 'fsdp')), may hold values from -0.6 to 1.45
- moment_in: float32 [768, 5376], P(('dp', 'fsdp')), may hold values from -0.55 to 0.55
- moment_out: float32 [3840, 768], P(('dp', 'fsdp')), may hold values from -0.55 to 0.55
- moment_vectors: float32 [12, 768], P(None, ('dp', 'fsdp')), may hold values from -1.5 to 1.5
- square_in: float32 [768, 5376], P(('dp', 'fsdp')), may hold values from 0.001 to 0.004
- square_out: float32 [3840, 768], P(('dp', 'fsdp')), may hold values from 0.001 to 0.004
- square_vectors: float32 [12, 768], P(None, ('dp', 'fsdp')), may hold values from 0.008 to 0.032
- step_count: int32 [1], replicated, may hold values from 1 to 20
Outputs:
- hidden_out: bfloat16 [20480, 768], P(('dp', 'fsdp'))
- logits: bfloat16 [32, 12, 640, 640], P(('dp', 'fsdp'))
- d_input: bfloat16 [20480, 768], P(('dp', 'fsdp'))
- d_prev: bfloat16 [32, 12, 640, 640], P(('dp', 'fsdp'))
- grad_weight_in: float32 [768, 5376], P(('dp', 'fsdp'))
- grad_weight_out: float32 [3840, 768], P(('dp', 'fsdp'))
- grad_vectors: float32 [12, 768], P(None, ('dp', 'fsdp'))
- new_moment_in: float32 [768, 5376], P(('dp', 'fsdp'))
- new_moment_out: float32 [3840, 768], P(('dp', 'fsdp'))
- new_moment_vectors: float32 [12, 768], P(None, ('dp', 'fsdp'))
- new_square_in: float32 [768, 5376], P(('dp', 'fsdp'))
- new_square_out: float32 [3840, 768], P(('dp', 'fsdp'))
- new_square_vectors: float32 [12, 768], P(None, ('dp', 'fsdp'))
- new_weight_in: float32 [768, 5376], P(('dp', 'fsdp'))
- new_weight_out: float32 [3840, 768], P(('dp', 'fsdp'))
- new_vectors: float32 [12, 768], P(None, ('dp', 'fsdp'))
- copy_weight_in: bfloat16 [768, 5376], P(('dp', 'fsdp'))
- copy_weight_out: bfloat16 [3840, 768], P(('dp', 'fsdp'))
- copy_vectors: bfloat16 [12, 768], P(None, ('dp', 'fsdp'))
- grad_norm: float32 [], replicated
Inputs may be any that keep to these rules, and one draw needn't show every extreme that they name: `segment_ids`: along each row the segment numbers never fall; no segment holds more than 320 slots.
All inputs are finite; a program needn't handle non-finite values.
Results may differ from a plain program's by a relative error of at most 0.012.
Values may be sent and summed in bfloat16 or wider, within the bound.
A program may use at most 192 MiB of HBM per device.

v0:
```python
import math
import jax
import jax.numpy as jnp
from jax import lax
from jax.sharding import PartitionSpec as P

PARAMS = 7087104
norm_eps = 1e-12
clip_scale = 1.0
beta_one = 0.9
beta_two = 0.999
adam_eps = 1e-08
rate_matrix = 0.06
rate_vector = 0.25
decay_matrix = 0.01
masked_fill = -1e30


def gelu_exact(upward):
    return jax.nn.gelu(upward, approximate=False)


def norm_rows(residual, gain_row, shift_row):
    centered = residual - jnp.mean(residual, axis=1, keepdims=True)
    scaling = lax.rsqrt(jnp.mean(centered * centered, axis=1, keepdims=True) + norm_eps)
    normed = centered * scaling
    return (normed * gain_row + shift_row, normed, scaling)


def norm_back(grad_after, normed, scaling, gain_row):
    scaled_grad = grad_after * gain_row
    return scaling * (
        scaled_grad
        - jnp.mean(scaled_grad, axis=1, keepdims=True)
        - normed * jnp.mean(scaled_grad * normed, axis=1, keepdims=True)
    )


def split_heads(matrix, head_count):
    return matrix.reshape(matrix.shape[0], head_count, -1)


def forward(weights, tokens, previous, same_doc):
    weight_in, weight_out, vectors = weights
    model_width = weight_out.shape[1]
    head_count = previous.shape[0]
    row_count = tokens.shape[0]
    score_scale = (model_width // head_count) ** (-0.5)
    vector_rows = vectors.astype(jnp.float32)
    projected = jnp.dot(tokens, weight_in[:, : 3 * model_width], preferred_element_type=jnp.float32)
    queries = (projected[:, :model_width] + vector_rows[4]).astype(jnp.bfloat16)
    keys_low = projected[:, model_width : 2 * model_width].astype(jnp.bfloat16)
    values_low = (projected[:, 2 * model_width :] + vector_rows[5]).astype(jnp.bfloat16)
    scores = jnp.einsum(
        "qhd,khd->hqk",
        split_heads(queries, head_count),
        split_heads(keys_low, head_count),
        preferred_element_type=jnp.float32,
    ) * score_scale + previous.astype(jnp.float32)
    masked = jnp.where(same_doc[None], scores, masked_fill)
    row_max = jnp.max(masked, axis=2, keepdims=True)
    expo_terms = jnp.exp(masked - row_max)
    totals = jnp.sum(expo_terms, axis=2, keepdims=True)
    attn_probs = expo_terms / totals
    log_sums = row_max + jnp.log(totals)
    mixed_heads = jnp.einsum(
        "hqk,khd->qhd",
        attn_probs.astype(jnp.bfloat16),
        split_heads(values_low, head_count),
        preferred_element_type=jnp.float32,
    )
    mixed_heads = mixed_heads.reshape(row_count, model_width).astype(jnp.bfloat16)
    first_sum = tokens.astype(jnp.float32) + (
        jnp.dot(mixed_heads, weight_out[:model_width], preferred_element_type=jnp.float32)
        + vector_rows[6]
    )
    hidden_one, normed_one, scale_one = norm_rows(first_sum, vector_rows[0], vector_rows[2])
    hidden_low = hidden_one.astype(jnp.bfloat16)
    upward = jnp.dot(
        hidden_low, weight_in[:, 3 * model_width :], preferred_element_type=jnp.float32
    ) + vector_rows[8:].reshape(-1)
    activated = gelu_exact(upward).astype(jnp.bfloat16)
    second_sum = hidden_one + (
        jnp.dot(activated, weight_out[model_width:], preferred_element_type=jnp.float32)
        + vector_rows[7]
    )
    output, normed_two, scale_two = norm_rows(second_sum, vector_rows[1], vector_rows[3])
    kept_values = (
        queries,
        keys_low,
        values_low,
        log_sums,
        mixed_heads,
        normed_one,
        scale_one,
        hidden_low,
        upward,
        activated,
        normed_two,
        scale_two,
    )
    return (output, scores, kept_values)


def backward(weights, kept_values, tokens, previous, same_doc, grad_hidden, grad_logits):
    weight_in, weight_out, vectors = weights
    (
        queries,
        keys_low,
        values_low,
        log_sums,
        mixed_heads,
        normed_one,
        scale_one,
        hidden_low,
        upward,
        activated,
        normed_two,
        scale_two,
    ) = kept_values
    model_width = weight_out.shape[1]
    head_count = previous.shape[0]
    row_count = tokens.shape[0]
    score_scale = (model_width // head_count) ** (-0.5)
    vector_rows = vectors.astype(jnp.float32)
    grad_output = grad_hidden.astype(jnp.float32)
    gain_two_grad = jnp.sum(grad_output * normed_two, axis=0)
    shift_two_grad = jnp.sum(grad_output, axis=0)
    grad_second = norm_back(grad_output, normed_two, scale_two, vector_rows[1])
    grad_down = grad_second.astype(jnp.bfloat16)
    bias_down_grad = jnp.sum(grad_down, axis=0, dtype=jnp.float32)
    down_grad = jnp.einsum("tf,td->fd", activated, grad_down, preferred_element_type=jnp.float32)
    grad_activated = jnp.einsum(
        "td,fd->tf", grad_down, weight_out[model_width:], preferred_element_type=jnp.float32
    )
    unused_value, gelu_pull = jax.vjp(gelu_exact, upward)
    grad_up = gelu_pull(grad_activated)[0].astype(jnp.bfloat16)
    bias_up_grad = jnp.sum(grad_up, axis=0, dtype=jnp.float32)
    up_grad = jnp.einsum("td,tf->df", hidden_low, grad_up, preferred_element_type=jnp.float32)
    grad_hidden_one = grad_second + jnp.einsum(
        "tf,df->td", grad_up, weight_in[:, 3 * model_width :], preferred_element_type=jnp.float32
    )
    gain_one_grad = jnp.sum(grad_hidden_one * normed_one, axis=0)
    shift_one_grad = jnp.sum(grad_hidden_one, axis=0)
    grad_first = norm_back(grad_hidden_one, normed_one, scale_one, vector_rows[0])
    grad_attn = grad_first.astype(jnp.bfloat16)
    bias_out_grad = jnp.sum(grad_attn, axis=0, dtype=jnp.float32)
    attn_grad = jnp.einsum("tc,td->cd", mixed_heads, grad_attn, preferred_element_type=jnp.float32)
    grad_mixed = jnp.einsum(
        "td,cd->tc", grad_attn, weight_out[:model_width], preferred_element_type=jnp.float32
    ).astype(jnp.bfloat16)
    head_queries = split_heads(queries, head_count)
    head_keys = split_heads(keys_low, head_count)
    head_values = split_heads(values_low, head_count)
    head_grad_mixed = split_heads(grad_mixed, head_count)
    scores = jnp.einsum(
        "qhd,khd->hqk", head_queries, head_keys, preferred_element_type=jnp.float32
    ) * score_scale + previous.astype(jnp.float32)
    attn_probs = jnp.exp(jnp.where(same_doc[None], scores, masked_fill) - log_sums)
    grad_probs = jnp.einsum(
        "qhd,khd->hqk", head_grad_mixed, head_values, preferred_element_type=jnp.float32
    )
    grad_scores = attn_probs * (
        grad_probs - jnp.sum(attn_probs * grad_probs, axis=2, keepdims=True)
    )
    grad_total = (grad_scores + grad_logits.astype(jnp.float32)).astype(jnp.bfloat16)
    grad_queries = (
        (
            jnp.einsum("hqk,khd->qhd", grad_total, head_keys, preferred_element_type=jnp.float32)
            * score_scale
        )
        .astype(jnp.bfloat16)
        .reshape(row_count, model_width)
    )
    grad_keys = (
        (
            jnp.einsum("hqk,qhd->khd", grad_total, head_queries, preferred_element_type=jnp.float32)
            * score_scale
        )
        .astype(jnp.bfloat16)
        .reshape(row_count, model_width)
    )
    grad_values = (
        jnp.einsum(
            "hqk,qhd->khd",
            attn_probs.astype(jnp.bfloat16),
            head_grad_mixed,
            preferred_element_type=jnp.float32,
        )
        .astype(jnp.bfloat16)
        .reshape(row_count, model_width)
    )
    grad_projected = jnp.concatenate([grad_queries, grad_keys, grad_values], axis=1)
    qkv_grad = jnp.einsum("td,tc->dc", tokens, grad_projected, preferred_element_type=jnp.float32)
    grad_tokens = grad_first + jnp.einsum(
        "tc,dc->td",
        grad_projected,
        weight_in[:, : 3 * model_width],
        preferred_element_type=jnp.float32,
    )
    small_rows = jnp.stack(
        [
            gain_one_grad,
            gain_two_grad,
            shift_one_grad,
            shift_two_grad,
            jnp.sum(grad_queries, axis=0, dtype=jnp.float32),
            jnp.sum(grad_values, axis=0, dtype=jnp.float32),
            bias_out_grad,
            bias_down_grad,
        ]
    )
    small_grads = jnp.concatenate([small_rows, bias_up_grad.reshape(-1, model_width)], axis=0)
    return (
        jnp.concatenate([qkv_grad, up_grad], axis=1),
        jnp.concatenate([attn_grad, down_grad], axis=0),
        small_grads,
        grad_tokens.astype(jnp.bfloat16),
        grad_total,
    )


def adam_update(master, moment, square, gradient, factor, step_value, step_rate, decay_rate):
    clipped = gradient * factor
    new_moment = beta_one * moment + (1.0 - beta_one) * clipped
    new_square = beta_two * square + (1.0 - beta_two) * clipped * clipped
    fixed_moment = new_moment / (1.0 - jnp.power(beta_one, step_value))
    fixed_square = new_square / (1.0 - jnp.power(beta_two, step_value))
    updated = master - step_rate * (
        fixed_moment / (jnp.sqrt(fixed_square) + adam_eps) + decay_rate * master
    )
    return (clipped, new_moment, new_square, updated)


def body(
    hidden_in,
    prev_logits,
    segment_ids,
    d_hidden,
    d_logits,
    weight_in,
    weight_out,
    vectors,
    moment_in,
    moment_out,
    moment_vectors,
    square_in,
    square_out,
    square_vectors,
    step_count,
):
    low_in = weight_in.astype(jnp.bfloat16)
    low_out = weight_out.astype(jnp.bfloat16)
    low_small = vectors.astype(jnp.bfloat16)
    gathered = (
        lax.all_gather(low_in, ("dp", "fsdp"), axis=0, tiled=True),
        lax.all_gather(low_out, ("dp", "fsdp"), axis=0, tiled=True),
        lax.all_gather(low_small, ("dp", "fsdp"), axis=1, tiled=True),
    )
    segments = segment_ids[0]
    same_doc = segments[:, None] == segments[None, :]
    previous = prev_logits[0]
    output, scores, kept_values = forward(gathered, hidden_in, previous, same_doc)
    regathered = (
        lax.all_gather(low_in, ("dp", "fsdp"), axis=0, tiled=True),
        lax.all_gather(low_out, ("dp", "fsdp"), axis=0, tiled=True),
        lax.all_gather(low_small, ("dp", "fsdp"), axis=1, tiled=True),
    )
    unused_out, unused_scores, again_values = forward(regathered, hidden_in, previous, same_doc)
    full_in, full_out, full_small, grad_tokens, grad_prev = backward(
        regathered, again_values, hidden_in, previous, same_doc, d_hidden, d_logits[0]
    )
    owned_in, owned_out, owned_small = (
        lax.psum_scatter(full_in, ("dp", "fsdp"), scatter_dimension=0, tiled=True),
        lax.psum_scatter(full_out, ("dp", "fsdp"), scatter_dimension=0, tiled=True),
        lax.psum_scatter(full_small, ("dp", "fsdp"), scatter_dimension=1, tiled=True),
    )
    local_squares = (
        jnp.sum(owned_in * owned_in)
        + jnp.sum(owned_out * owned_out)
        + jnp.sum(owned_small * owned_small)
    )
    total_squares = lax.psum(local_squares, ("dp", "fsdp"))
    grad_norm = jnp.sqrt(total_squares)
    threshold = clip_scale * math.sqrt(PARAMS)
    factor = jnp.minimum(1.0, threshold / (grad_norm + 1e-06))
    step_value = step_count[0].astype(jnp.float32)
    clip_in, moment_one, square_one, updated_in = adam_update(
        weight_in, moment_in, square_in, owned_in, factor, step_value, rate_matrix, decay_matrix
    )
    clip_out, moment_two, square_two, updated_out = adam_update(
        weight_out, moment_out, square_out, owned_out, factor, step_value, rate_matrix, decay_matrix
    )
    clip_small, moment_three, square_three, updated_small = adam_update(
        vectors, moment_vectors, square_vectors, owned_small, factor, step_value, rate_vector, 0.0
    )
    return (
        output.astype(jnp.bfloat16),
        scores.astype(jnp.bfloat16)[None],
        grad_tokens,
        grad_prev[None],
        clip_in,
        clip_out,
        clip_small,
        moment_one,
        moment_two,
        moment_three,
        square_one,
        square_two,
        square_three,
        updated_in,
        updated_out,
        updated_small,
        updated_in.astype(jnp.bfloat16),
        updated_out.astype(jnp.bfloat16),
        updated_small.astype(jnp.bfloat16),
        grad_norm,
    )


def solution(mesh):
    return jax.shard_map(
        body,
        mesh=mesh,
        in_specs=(
            P(("dp", "fsdp"), None),
            P(("dp", "fsdp"), None, None, None),
            P(("dp", "fsdp"), None),
            P(("dp", "fsdp"), None),
            P(("dp", "fsdp"), None, None, None),
            P(("dp", "fsdp"), None),
            P(("dp", "fsdp"), None),
            P(None, ("dp", "fsdp")),
            P(("dp", "fsdp"), None),
            P(("dp", "fsdp"), None),
            P(None, ("dp", "fsdp")),
            P(("dp", "fsdp"), None),
            P(("dp", "fsdp"), None),
            P(None, ("dp", "fsdp")),
            P(),
        ),
        out_specs=(
            P(("dp", "fsdp"), None),
            P(("dp", "fsdp"), None, None, None),
            P(("dp", "fsdp"), None),
            P(("dp", "fsdp"), None, None, None),
            P(("dp", "fsdp"), None),
            P(("dp", "fsdp"), None),
            P(None, ("dp", "fsdp")),
            P(("dp", "fsdp"), None),
            P(("dp", "fsdp"), None),
            P(None, ("dp", "fsdp")),
            P(("dp", "fsdp"), None),
            P(("dp", "fsdp"), None),
            P(None, ("dp", "fsdp")),
            P(("dp", "fsdp"), None),
            P(("dp", "fsdp"), None),
            P(None, ("dp", "fsdp")),
            P(("dp", "fsdp"), None),
            P(("dp", "fsdp"), None),
            P(None, ("dp", "fsdp")),
            P(),
        ),
        check_vma=False,
    )
```

profile of v0, /device:TPU:0, one launch (start us, length us, event | category | flops | bytes accessed | tf_op | source)
XLA Modules:
  0.0 645.5 jit_solution(6729992086085996024)
XLA Ops:
  11.5 71.6 %all-gather = bf16[32,24,12]{1,2,0:T(8,128)(2,1)S(1)} all-gather(bf16[1,24,12]{1,2,0:T(8,128)(2,1)S(1)} %convert_bitcast_fusion.1), channel_id=1, replica_groups=mesh['dp'=4,'fsdp'=8] {'dp','fsdp'}, dimensions={0}, use_global_device_ids=true | all-gather | bytes 19008 | tf_op jit(solution)/shard_map/all_gather | solution.py:258
  83.5 14.0 %copy.85 = bf16[1,12,640,640]{2,3,1,0:T(8,128)(2,1)} copy(bf16[1,12,640,640]{3,2,1,0:T(8,128)(2,1)} %param.16) | data formatting | bytes 19660800 | tf_op args[1]
  98.0 4.5 fusion.34
  105.2 1.9 copy.82
  107.1 11.9 %select_reduce_fusion = (f32[12,640]{1,0:T(8,128)S(1)}, f32[12,640,640]{1,2,0:T(8,128)}) fusion(pred[640,640]{0,1:T(8,128)(4,1)S(1)} %broadcast_compare_fusion, bf16[1,12,640,640]{2,3,1,0:T(8,128)(2,1)} %copy.85, bf16[640,12,64]{0,2,1:T(8,128)(2,1)S(1)} %bitcast.63, bf16[640,12,64]{0,2,1:T(8,128)(2,1)S(1)} %bitcast.61), kind=kOutput, calls=%fused_computation.11 | convolution fusion | flops 653713920 | bytes 31897600 | tf_op jit(solution)/shard_map/qhd,khd->hqk/dot_general | solution.py:54
  119.0 17.7 %convert_bitcast_fusion = (bf16[1,12,640,640]{2,3,1,0:T(8,128)(2,1)}, f32[12,640]{1,0:T(8,128)S(1)}) fusion(f32[12,640,640]{1,2,0:T(8,128)} %get-tuple-element.143, f32[12,640]{1,0:T(8,128)S(1)} %get-tuple-element.142, pred[640,640]{0,1:T(8,128)(4,1)S(1)} %broadcast_compare_fusion), kind=kLoop, calls=%fused_computation.18 | loop fusion | flops 19653120 | bytes 29962240 | tf_op jit(solution)/shard_map/broadcast_in_dim | solution.py:299
  136.8 10.8 %fusion.55 = bf16[12,64,640]{2,1,0:T(8,128)(2,1)} fusion(bf16[640,12,64]{0,2,1:T(8,128)(2,1)S(1)} %bitcast.67, f32[12,640,640]{1,2,0:T(8,128)} %get-tuple-element.143, f32[12,640]{1,0:T(8,128)S(1)} %get-tuple-element.138, f32[12,640]{1,0:T(8,128)S(1)} %get-tuple-element.142, pred[640,640]{0,1:T(8,128)(4,1)S(1)} %broadcast_compare_fusion), kind=kOutput, calls=%fused_computation.92 | convolution fusion | flops 649297920 | bytes 22097920 | tf_op jit(solution)/shard_map/hqk,khd->qhd/dot_general | solution.py:66
  147.6 14.3 %all-gather.6.cloned.1.call-done = bf16[3840,768]{1,0:T(8,128)(2,1)} async-done(((bf16[120,768]{1,0:T(8,128)(2,1)}), bf16[3840,768]{1,0:T(8,128)(2,1)}) %all-gather.6.cloned.1.call-update) | async-done | bytes 5898256 | tf_op jit(solution)/shard_map/all_gather | solution.py:257
  161.9 3.1 fusion.86
  165.4 23.9 %multiply_convert_fusion = (bf16[640,3072]{1,0:T(8,128)(2,1)S(1)}, f32[640,3072]{1,0:T(8,128)}, f32[640,3072]{1,0:T(8,128)}) fusion(f32[3072]{0:T(1024)S(1)} %add.219, bf16[768,5376]{1,0:T(8,128)(2,1)} %all-gather.4.cloned.1.call-done, f32[640,768]{1,0:T(8,128)S(1)} %get-tuple-element.145, f32[768]{0:T(1024)S(1)} %get-tuple-element.111, ...), kind=kOutput, calls=%fused_computation.27 | convolution fusion | flops 3152117760 | bytes 26369024 | tf_op jit(solution)/shard_map/dot_general | solution.py:79
  189.3 3.4 fusion.87
  195.9 6.4 fusion.69
  202.3 10.9 %convert_reduce_fusion = (f32[3072]{0:T(1024)S(1)}, bf16[640,3072]{1,0:T(8,128)(2,1)S(1)}) fusion(f32[640,3072]{1,0:T(8,128)} %get-tuple-element.136, bf16[3840,768]{1,0:T(8,128)(2,1)} %all-gather.6.cloned.1.call-done, f32[640,768]{1,0:T(8,128)S(1)} %get-tuple-element.132, f32[640,3072]{1,0:T(8,128)} %get-tuple-element.146, f32[3072]{0:T(1024)S(1)} %add.219), kind=kOutput, calls=%fused_computation.25 | convolution fusion | flops 3053810688 | bytes 26370048 | tf_op jit(solution)/shard_map/td,fd->tf/dot_general | solution.py:133
  213.3 3.8 multiply_reduce_fusion.1
  219.0 2.5 fusion.66
  221.5 9.5 %pad_maximum_fusion.1 = f32[3840,768]{1,0:T(8,128)} fusion(f32[3072,768]{1,0:T(8,128)} %fusion.69, f32[768,768]{1,0:T(8,128)} %fusion.66), kind=kLoop, calls=%fused_computation.13 | loop fusion | flops 2949120 | bytes 23592960 | tf_op jit(solution)/shard_map/concatenate | solution.py:216
  231.1 15.4 %copy.88 = bf16[1,12,640,640]{2,3,1,0:T(8,128)(2,1)} copy(bf16[1,12,640,640]{3,2,1,0:T(8,128)(2,1)} %param.19) | data formatting | bytes 19660800 | tf_op args[4]
  246.5 3.0 convolution_convert_fusion
  250.9 28.2 %fusion.1 = bf16[12,640,640]{1,2,0:T(8,128)(2,1)} fusion(f32[12,640,640]{1,2,0:T(8,128)} %get-tuple-element.143, bf16[1,12,640,640]{2,3,1,0:T(8,128)(2,1)} %copy.88, f32[12,640]{1,0:T(8,128)S(1)} %log_add_fusion, pred[640,640]{0,1:T(8,128)(4,1)S(1)} %broadcast_compare_fusion, bf16[640,12,64]{0,2,1:T(8,128)(2,1)} %bitcast.73, bf16[640,12,64]{0,2,1:T(8,128)(2,1)} %bitcast.68), kind=kOutput, calls=%fused_computation.2 | convolution fusion | flops 1307451520 | bytes 41728000 | tf_op jit(solution)/shard_map/sub | solution.py:164
  279.2 5.8 convert_reduce_fusion.5
  287.0 3.2 multiply_convert_fusion.1
  290.2 11.5 %convert_reduce_fusion.4 = (f32[12,64]{1,0:T(8,128)S(1)}, bf16[12,64,640]{2,1,0:T(8,128)(2,1)S(1)}) fusion(bf16[640,12,64]{0,2,1:T(8,128)(2,1)S(1)} %bitcast.74, f32[12,640,640]{1,2,0:T(8,128)} %get-tuple-element.143, f32[12,640]{1,0:T(8,128)S(1)} %log_add_fusion, pred[640,640]{0,1:T(8,128)(4,1)S(1)} %broadcast_compare_fusion), kind=kOutput, calls=%fused_computation.73 | convolution fusion | flops 645364992 | bytes 22070272 | tf_op jit(solution)/shard_map/hqk,qhd->khd/dot_general | solution.py:184
  302.8 7.9 %convolution_bitcast_fusion = f32[768,2304]{0,1:T(8,128)} fusion(bf16[640,768]{1,0:T(8,128)(2,1)S(1)} %copy-done.29, bf16[640,768]{0,1:T(8,128)(2,1)S(1)} %bitcast.81, bf16[640,768]{0,1:T(8,128)(2,1)S(1)} %bitcast.69, bf16[640,768]{0,1:T(8,128)(2,1)S(1)} %bitcast.65), kind=kOutput, calls=%fused_computation.41 | convolution fusion | flops 2273771520 | bytes 11010048 | tf_op jit(solution)/shard_map/td,tc->dc/dot_general | solution.py:194
  310.7 8.2 %copy.92 = f32[768,2304]{1,0:T(8,128)} copy(f32[768,2304]{0,1:T(8,128)} %convolution_bitcast_fusion) | data formatting | bytes 14155776 | tf_op jit(solution)/shard_map/td,tc->dc/dot_general | solution.py:194
  318.9 6.6 %fusion.75 = f32[768,3072]{1,0:T(8,128)S(1)} fusion(bf16[640,3072]{1,0:T(8,128)(2,1)} %copy-done.9, f32[640,768]{1,0:T(8,128)S(1)} %get-tuple-element.145, f32[768]{0:T(1024)S(1)} %get-tuple-element.111, f32[768]{0:T(1024)S(1)} %get-tuple-element.112, f32[640]{0:T(1024)S(1)} %add_rsqrt_fusion.1, f32[640]{0:T(1024)S(1)} %broadcast_multiply_fusion.7), kind=kOutput, calls=%fused_computation.145 | convolution fusion | flops 3022356480 | bytes 15346688 | tf_op jit(solution)/shard_map/td,tf->df/dot_general | solution.py:139
  325.5 6.0 pad_maximum_fusion
  332.5 13.9 %copy.94 = bf16[1,12,640,640]{3,2,1,0:T(8,128)(2,1)} copy(bf16[1,12,640,640]{2,3,1,0:T(8,128)(2,1)} %bitcast.60) | data formatting | bytes 19660800
  346.4 39.7 %all-reduce = f32[12,768]{1,0:T(8,128)S(1)} all-reduce(f32[12,768]{1,0:T(8,128)S(1)} %concatenate.15), channel_id=4, replica_groups=mesh['dp'=4,'fsdp'=8] {'dp','fsdp'}, use_global_device_ids=true, to_apply=%region_24.25.clone | all-reduce | flops 9216 | bytes 73728
  386.9 6.0 add_convert_fusion.1
  394.6 180.7 %reduce-scatter.4.cloned.1.call-done = f32[24,5376]{1,0:T(8,128)} async-done(((f32[768,5376]{1,0:T(8,128)}), f32[24,5376]{1,0:T(8,128)}) %reduce-scatter.4.cloned.1.call-update) | async-done | bytes 516112 | tf_op jit(solution)/shard_map/reduce_scatter | solution.py:274
  579.2 13.9 %copy.93 = bf16[1,12,640,640]{3,2,1,0:T(8,128)(2,1)} copy(bf16[1,12,640,640]{2,3,1,0:T(8,128)(2,1)} %get-tuple-element.137) | data formatting | bytes 19660800
  593.2 39.3 %psum.7 = f32[]{:T(128)} all-reduce(f32[]{:T(128)S(6)} %add.235), channel_id=1, replica_groups=mesh['dp'=4,'fsdp'=8] {'dp','fsdp'}, use_global_device_ids=true, to_apply=%region_26.27 | all-reduce | flops 1 | bytes 8 | tf_op jit(solution)/shard_map/psum | solution.py:283
  (127 shorter events, 26.3 us)
Async XLA Ops:
  7.2 90.8 %all-gather.4.cloned.1.call-start = ((), (), s32[]{:S(2)}) async-start(), calls=%async_computation.2 | async-start | bytes 8515584 | tf_op jit(solution)/shard_map/all_gather | solution.py:256
  9.0 152.9 %all-gather.6.cloned.1.call-start = ((), (), s32[]{:S(2)}) async-start(), calls=%async_computation.3 | async-start | bytes 6082560 | tf_op jit(solution)/shard_map/all_gather | solution.py:257
  10.8 382.1 %reduce-scatter.6.cloned.1.call-start = ((), (), s32[]{:S(2)}) async-start(), calls=%async_computation.5 | async-start | bytes 12165120 | tf_op jit(solution)/shard_map/reduce_scatter | solution.py:275
  83.5 14.0 %copy-start.27 = (s32[1,640]{1,0:T(1,128)S(1)}, s32[1,640]{1,0:T(1,128)}, u32[]{:S(2)}) copy-start(s32[1,640]{1,0:T(1,128)} %param.17) | copy-start | bytes 7684
  83.5 14.4 %copy-start.28 = (bf16[640,768]{1,0:T(8,128)(2,1)S(1)}, bf16[640,768]{1,0:T(8,128)(2,1)}, u32[]{:S(2)}) copy-start(bf16[640,768]{1,0:T(8,128)(2,1)} %param.15) | copy-start | bytes 2949124
  104.5 14.5 %copy-start.4 = (bf16[640,768]{0,1:T(8,128)(2,1)}, bf16[640,768]{0,1:T(8,128)(2,1)S(1)}, u32[]{:S(2)}) copy-start(bf16[640,768]{0,1:T(8,128)(2,1)S(1)} %copy.83) | copy-start | bytes 2949124
  105.2 13.9 %copy-start.2 = (bf16[640,768]{0,1:T(8,128)(2,1)}, bf16[640,768]{0,1:T(8,128)(2,1)S(1)}, u32[]{:S(2)}) copy-start(bf16[640,768]{0,1:T(8,128)(2,1)S(1)} %copy.84) | copy-start | bytes 2949124
  107.1 29.7 %copy-start.16 = (bf16[640,768]{0,1:T(8,128)(2,1)}, bf16[640,768]{0,1:T(8,128)(2,1)S(1)}, u32[]{:S(2)}) copy-start(bf16[640,768]{0,1:T(8,128)(2,1)S(1)} %copy.82) | copy-start | bytes 2949124
  161.9 27.4 %slice-start.2 = ((s8[5898240]{0:T(1024)(128)(4,1)}), s8[4194304]{0:T(1024)(128)(4,1)S(1)}, s32[]{:S(2)}) async-start(s8[5898240]{0:T(1024)(128)(4,1)} %bitcast.79), calls=%async_computation.8 | async-start | bytes 8388608
  165.4 23.9 %slice-start.3 = ((s8[5898240]{0:T(1024)(128)(4,1)}), s8[1703936]{0:T(1024)(128)(4,1)S(1)}, s32[]{:S(2)}) async-start(s8[5898240]{0:T(1024)(128)(4,1)} %bitcast.79), calls=%async_computation.9 | async-start | bytes 3407872
  195.9 17.3 %slice-start = ((s8[8257536]{0:T(1024)(128)(4,1)}), s8[4194304]{0:T(1024)(128)(4,1)S(1)}, s32[]{:S(2)}) async-start(s8[8257536]{0:T(1024)(128)(4,1)} %bitcast.77), calls=%async_computation.6 | async-start | bytes 8388608
  202.3 10.9 %slice-start.1 = ((s8[8257536]{0:T(1024)(128)(4,1)}), s8[4063232]{0:T(1024)(128)(4,1)S(1)}, s32[]{:S(2)}) async-start(s8[8257536]{0:T(1024)(128)(4,1)} %bitcast.77), calls=%async_computation.7 | async-start | bytes 8126464
  231.0 344.4 %reduce-scatter.4.cloned.1.call-start = ((), (), s32[]{:S(2)}) async-start(), calls=%async_computation.4 | async-start | bytes 17031168 | tf_op jit(solution)/shard_map/reduce_scatter | solution.py:274
  250.9 28.3 %copy-start.3 = (bf16[640,768]{0,1:T(8,128)(2,1)S(1)}, bf16[640,768]{0,1:T(8,128)(2,1)}, u32[]{:S(2)}) copy-start(bf16[640,768]{0,1:T(8,128)(2,1)} %copy-done.2) | copy-start | bytes 2949124
  279.2 7.6 %copy-start = (bf16[12,640,640]{1,2,0:T(8,128)(2,1)S(1)}, bf16[12,640,640]{1,2,0:T(8,128)(2,1)}, u32[]{:S(2)}) copy-start(bf16[12,640,640]{1,2,0:T(8,128)(2,1)} %fusion.1) | copy-start | bytes 29491204
  279.2 7.8 %copy-start.5 = (bf16[640,768]{0,1:T(8,128)(2,1)S(1)}, bf16[640,768]{0,1:T(8,128)(2,1)}, u32[]{:S(2)}) copy-start(bf16[640,768]{0,1:T(8,128)(2,1)} %copy-done.4) | copy-start | bytes 2949124
  287.0 14.8 %copy-start.10 = (bf16[12,64,640]{2,1,0:T(8,128)(2,1)}, bf16[12,64,640]{2,1,0:T(8,128)(2,1)S(1)}, u32[]{:S(2)}) copy-start(bf16[12,64,640]{2,1,0:T(8,128)(2,1)S(1)} %get-tuple-element.151) | copy-start | bytes 2949124
  290.2 11.6 %copy-start.17 = (bf16[12,64,640]{2,1,0:T(8,128)(2,1)}, bf16[12,64,640]{2,1,0:T(8,128)(2,1)S(1)}, u32[]{:S(2)}) copy-start(bf16[12,64,640]{2,1,0:T(8,128)(2,1)S(1)} %multiply_convert_fusion.1) | copy-start | bytes 2949124
  290.2 12.5 %copy-start.29 = (bf16[640,768]{1,0:T(8,128)(2,1)S(1)}, bf16[640,768]{1,0:T(8,128)(2,1)}, u32[]{:S(2)}) copy-start(bf16[640,768]{1,0:T(8,128)(2,1)} %param.15) | copy-start | bytes 2949124
  332.4 54.4 %copy-start.7 = (f32[640,768]{1,0:T(8,128)S(1)}, f32[640,768]{1,0:T(8,128)}, u32[]{:S(2)}) copy-start(f32[640,768]{1,0:T(8,128)} %copy-done.6) | copy-start | bytes 5898244
  332.5 54.4 %copy-start.11 = (bf16[12,64,640]{2,1,0:T(8,128)(2,1)S(1)}, bf16[12,64,640]{2,1,0:T(8,128)(2,1)}, u32[]{:S(2)}) copy-start(bf16[12,64,640]{2,1,0:T(8,128)(2,1)} %copy-done.10) | copy-start | bytes 2949124
  386.2 6.7 %copy-start.24 = (f32[12,768]{1,0:T(8,128)}, f32[12,768]{1,0:T(8,128)S(1)}, u32[]{:S(2)}) copy-start(f32[12,768]{1,0:T(8,128)S(1)} %all-reduce) | copy-start | bytes 110596
  579.1 54.1 %copy-start.25 = (f32[12,24]{1,0:T(8,128)S(1)}, f32[12,24]{1,0:T(8,128)}, u32[]{:S(2)}) copy-start(f32[12,24]{1,0:T(8,128)} %param.22) | copy-start | bytes 3460
  579.1 54.1 %copy-start.26 = (f32[12,24]{1,0:T(8,128)S(1)}, f32[12,24]{1,0:T(8,128)}, u32[]{:S(2)}) copy-start(f32[12,24]{1,0:T(8,128)} %param.28) | copy-start | bytes 3460
  579.1 55.6 %copy-start.14 = (f32[120,768]{1,0:T(8,128)S(1)}, f32[120,768]{1,0:T(8,128)}, u32[]{:S(2)}) copy-start(f32[120,768]{1,0:T(8,128)} %param.21) | copy-start | bytes 1105924
  579.1 55.6 %copy-start.15 = (f32[120,768]{1,0:T(8,128)S(1)}, f32[120,768]{1,0:T(8,128)}, u32[]{:S(2)}) copy-start(f32[120,768]{1,0:T(8,128)} %reduce-scatter.6.cloned.1.call-done) | copy-start | bytes 1105924
  579.2 55.6 %copy-start.22 = (f32[120,768]{1,0:T(8,128)S(1)}, f32[120,768]{1,0:T(8,128)}, u32[]{:S(2)}) copy-start(f32[120,768]{1,0:T(8,128)} %param.27) | copy-start | bytes 1105924
  579.2 55.5 %copy-start.23 = (f32[120,768]{1,0:T(8,128)S(1)}, f32[120,768]{1,0:T(8,128)}, u32[]{:S(2)}) copy-start(f32[120,768]{1,0:T(8,128)} %param.24) | copy-start | bytes 1105924
  579.2 56.8 %copy-start.12 = (f32[24,5376]{1,0:T(8,128)S(1)}, f32[24,5376]{1,0:T(8,128)}, u32[]{:S(2)}) copy-start(f32[24,5376]{1,0:T(8,128)} %param.20) | copy-start | bytes 1548292
  579.2 56.8 %copy-start.13 = (f32[24,5376]{1,0:T(8,128)S(1)}, f32[24,5376]{1,0:T(8,128)}, u32[]{:S(2)}) copy-start(f32[24,5376]{1,0:T(8,128)} %reduce-scatter.4.cloned.1.call-done) | copy-start | bytes 1548292
  579.2 56.8 %copy-start.20 = (f32[24,5376]{1,0:T(8,128)S(1)}, f32[24,5376]{1,0:T(8,128)}, u32[]{:S(2)}) copy-start(f32[24,5376]{1,0:T(8,128)} %param.26) | copy-start | bytes 1548292
  579.2 56.8 %copy-start.21 = (f32[24,5376]{1,0:T(8,128)S(1)}, f32[24,5376]{1,0:T(8,128)}, u32[]{:S(2)}) copy-start(f32[24,5376]{1,0:T(8,128)} %param.23) | copy-start | bytes 1548292
  (7 other events, 25.6 us)
Sparse Core Ops, SparseCore 0:
  11.6 80.3 all-gather.3
  95.5 66.3 all-gather.5
  231.2 146.7 reduce-scatter.5
  385.2 190.0 reduce-scatter.3
where the time goes:
time: 656 us; the launch traced here: 646 us
  waiting for transfers between devices  195 us (30%)
  matrix products  154 us (23%)
  blocking collectives  151 us (23%)
  local copies, waits for them, and re-layouts  75.2 us (11%)
  other arithmetic  51.4 us (8%)
  between operations  19.3 us (3%)
    reduce_scatter x1, waiting for transfers between devices, body(): lax.psum_scatter(full_in, ('dp', 'fsdp'), scatter_dimension=0, tiled=True)  181 us
    all_gather x1, blocking collectives, body(): lax.all_gather(low_small, ('dp', 'fsdp'), axis=1, tiled=True)  71.6 us
    unnamed x74, local copies, waits for them, and re-layouts  61.7 us
    unnamed x1, blocking collectives  39.7 us
    psum x1, blocking collectives, body(): total_squares = lax.psum(local_squares, ('dp', 'fsdp'))  39.3 us
    sub x1, matrix products, backward(): grad_probs - jnp.sum(attn_probs * grad_probs, axis=2, keepdims=True)  28.2 us
    dot_general x1, matrix products, forward(): jnp.dot(hidden_low, weight_in[:, 3 * model_width:], preferred_element_typ...  23.9 us
    broadcast_in_dim x1, other arithmetic, body(): scores.astype(jnp.bfloat16)[None]  17.7 us
  transfers between devices with their start and end apart: 4, of which 2 were waited for; matrix products, arithmetic and copies ran while one was open for 29% of the time, Pallas kernels for 0%

commit v1 on v0

--- a/solution.py
+++ b/solution.py
@@ -280,7 +280,7 @@
         + jnp.sum(owned_out * owned_out)
         + jnp.sum(owned_small * owned_small)
     )
-    total_squares = lax.psum(local_squares, ("dp", "fsdp"))
+    total_squares = lax.psum(lax.psum(local_squares, axis_name="fsdp"), axis_name="dp")
     grad_norm = jnp.sqrt(total_squares)
     threshold = clip_scale * math.sqrt(PARAMS)
     factor = jnp.minimum(1.0, threshold / (grad_norm + 1e-06))

time: 656 us -> 657 us (level)
  waiting for transfers between devices: 195 us -> 209 us
  blocking collectives: 151 us -> 139 us
    reduce_scatter x1, waiting for transfers between devices: 181 us -> 194 us  [body(): lax.psum_scatter(full_in, ('dp', 'fsdp'), scatter_dimension=0, tiled=True)]
    psum x1 -> x2, blocking collectives: 39.3 us -> 26.5 us  [the longest x1 20.2 us: body(): lax.psum(local_squares, axis_name='fsdp')]
  transfers between devices with their start and end apart: 4 -> 4, of which waited for: 2 -> 2; matrix products, arithmetic and copies ran while one was open for 29% -> 27% of each run, Pallas kernels for 0% -> 0%
where the time goes in v1:
time: 657 us; the launch traced here: 647 us
  waiting for transfers between devices  209 us (32%)
  matrix products  154 us (23%)
  blocking collectives  139 us (21%)
  local copies, waits for them, and re-layouts  75.1 us (11%)
  other arithmetic  51.3 us (8%)
  between operations  19.4 us (3%)
    reduce_scatter x1, waiting for transfers between devices, body(): lax.psum_scatter(full_in, ('dp', 'fsdp'), scatter_dimension=0, tiled=True)  194 us
    all_gather x1, blocking collectives, body(): lax.all_gather(low_small, ('dp', 'fsdp'), axis=1, tiled=True)  71.6 us
    unnamed x74, local copies, waits for them, and re-layouts  61.6 us
    unnamed x1, blocking collectives  40.6 us
    sub x1, matrix products, backward(): grad_probs - jnp.sum(attn_probs * grad_probs, axis=2, keepdims=True)  28.2 us
    dot_general x1, matrix products, forward(): jnp.dot(hidden_low, weight_in[:, 3 * model_width:], preferred_element_typ...  23.9 us
    psum x1, blocking collectives, body(): lax.psum(local_squares, axis_name='fsdp')  20.2 us
    broadcast_in_dim x1, other arithmetic, body(): scores.astype(jnp.bfloat16)[None]  17.7 us
  transfers between devices with their start and end apart: 4, of which 2 were waited for; matrix products, arithmetic and copies ran while one was open for 27% of the time, Pallas kernels for 0%

profile of v1, /device:TPU:0, one launch (start us, length us, event | category | flops | bytes accessed | tf_op | source)
XLA Modules:
  0.0 647.3 jit_solution(1729423751871745051)
XLA Ops:
  11.5 71.6 %all-gather = bf16[32,24,12]{1,2,0:T(8,128)(2,1)S(1)} all-gather(bf16[1,24,12]{1,2,0:T(8,128)(2,1)S(1)} %convert_bitcast_fusion.1), channel_id=1, replica_groups=mesh['dp'=4,'fsdp'=8] {'dp','fsdp'}, dimensions={0}, use_global_device_ids=true | all-gather | bytes 19008 | tf_op jit(solution)/shard_map/all_gather | solution.py:258
  83.5 14.0 %copy.85 = bf16[1,12,640,640]{2,3,1,0:T(8,128)(2,1)} copy(bf16[1,12,640,640]{3,2,1,0:T(8,128)(2,1)} %param.16) | data formatting | bytes 19660800 | tf_op args[1]
  98.0 4.5 fusion.34
  107.1 11.9 %select_reduce_fusion = (f32[12,640]{1,0:T(8,128)S(1)}, f32[12,640,640]{1,2,0:T(8,128)}) fusion(pred[640,640]{0,1:T(8,128)(4,1)S(1)} %broadcast_compare_fusion, bf16[1,12,640,640]{2,3,1,0:T(8,128)(2,1)} %copy.85, bf16[640,12,64]{0,2,1:T(8,128)(2,1)S(1)} %bitcast.63, bf16[640,12,64]{0,2,1:T(8,128)(2,1)S(1)} %bitcast.61), kind=kOutput, calls=%fused_computation.11 | convolution fusion | flops 653713920 | bytes 31897600 | tf_op jit(solution)/shard_map/qhd,khd->hqk/dot_general | solution.py:54
  119.0 17.7 %convert_bitcast_fusion = (bf16[1,12,640,640]{2,3,1,0:T(8,128)(2,1)}, f32[12,640]{1,0:T(8,128)S(1)}) fusion(f32[12,640,640]{1,2,0:T(8,128)} %get-tuple-element.143, f32[12,640]{1,0:T(8,128)S(1)} %get-tuple-element.142, pred[640,640]{0,1:T(8,128)(4,1)S(1)} %broadcast_compare_fusion), kind=kLoop, calls=%fused_computation.18 | loop fusion | flops 19653120 | bytes 29962240 | tf_op jit(solution)/shard_map/broadcast_in_dim | solution.py:299
  136.8 10.8 %fusion.55 = bf16[12,64,640]{2,1,0:T(8,128)(2,1)} fusion(bf16[640,12,64]{0,2,1:T(8,128)(2,1)S(1)} %bitcast.67, f32[12,640,640]{1,2,0:T(8,128)} %get-tuple-element.143, f32[12,640]{1,0:T(8,128)S(1)} %get-tuple-element.138, f32[12,640]{1,0:T(8,128)S(1)} %get-tuple-element.142, pred[640,640]{0,1:T(8,128)(4,1)S(1)} %broadcast_compare_fusion), kind=kOutput, calls=%fused_computation.92 | convolution fusion | flops 649297920 | bytes 22097920 | tf_op jit(solution)/shard_map/hqk,khd->qhd/dot_general | solution.py:66
  147.6 14.3 %all-gather.6.cloned.1.call-done = bf16[3840,768]{1,0:T(8,128)(2,1)} async-done(((bf16[120,768]{1,0:T(8,128)(2,1)}), bf16[3840,768]{1,0:T(8,128)(2,1)}) %all-gather.6.cloned.1.call-update) | async-done | bytes 5898256 | tf_op jit(solution)/shard_map/all_gather | solution.py:257
  161.9 3.1 fusion.86
  165.4 23.9 %multiply_convert_fusion = (bf16[640,3072]{1,0:T(8,128)(2,1)S(1)}, f32[640,3072]{1,0:T(8,128)}, f32[640,3072]{1,0:T(8,128)}) fusion(f32[3072]{0:T(1024)S(1)} %add.221, bf16[768,5376]{1,0:T(8,128)(2,1)} %all-gather.4.cloned.1.call-done, f32[640,768]{1,0:T(8,128)S(1)} %get-tuple-element.145, f32[768]{0:T(1024)S(1)} %get-tuple-element.111, ...), kind=kOutput, calls=%fused_computation.27 | convolution fusion | flops 3152117760 | bytes 26369024 | tf_op jit(solution)/shard_map/dot_general | solution.py:79
  189.3 3.4 fusion.87
  195.9 6.4 fusion.69
  202.3 10.9 %convert_reduce_fusion = (f32[3072]{0:T(1024)S(1)}, bf16[640,3072]{1,0:T(8,128)(2,1)S(1)}) fusion(f32[640,3072]{1,0:T(8,128)} %get-tuple-element.136, bf16[3840,768]{1,0:T(8,128)(2,1)} %all-gather.6.cloned.1.call-done, f32[640,768]{1,0:T(8,128)S(1)} %get-tuple-element.132, f32[640,3072]{1,0:T(8,128)} %get-tuple-element.146, f32[3072]{0:T(1024)S(1)} %add.221), kind=kOutput, calls=%fused_computation.25 | convolution fusion | flops 3053810688 | bytes 26370048 | tf_op jit(solution)/shard_map/td,fd->tf/dot_general | solution.py:133
  213.3 3.8 multiply_reduce_fusion.1
  219.0 2.5 fusion.66
  221.5 9.5 %pad_maximum_fusion.1 = f32[3840,768]{1,0:T(8,128)} fusion(f32[3072,768]{1,0:T(8,128)} %fusion.69, f32[768,768]{1,0:T(8,128)} %fusion.66), kind=kLoop, calls=%fused_computation.13 | loop fusion | flops 2949120 | bytes 23592960 | tf_op jit(solution)/shard_map/concatenate | solution.py:216
  231.1 15.4 %copy.88 = bf16[1,12,640,640]{2,3,1,0:T(8,128)(2,1)} copy(bf16[1,12,640,640]{3,2,1,0:T(8,128)(2,1)} %param.19) | data formatting | bytes 19660800 | tf_op args[4]
  246.5 3.0 convolution_convert_fusion
  250.9 28.2 %fusion.1 = bf16[12,640,640]{1,2,0:T(8,128)(2,1)} fusion(f32[12,640,640]{1,2,0:T(8,128)} %get-tuple-element.143, bf16[1,12,640,640]{2,3,1,0:T(8,128)(2,1)} %copy.88, f32[12,640]{1,0:T(8,128)S(1)} %log_add_fusion, pred[640,640]{0,1:T(8,128)(4,1)S(1)} %broadcast_compare_fusion, bf16[640,12,64]{0,2,1:T(8,128)(2,1)} %bitcast.73, bf16[640,12,64]{0,2,1:T(8,128)(2,1)} %bitcast.68), kind=kOutput, calls=%fused_computation.2 | convolution fusion | flops 1307451520 | bytes 41728000 | tf_op jit(solution)/shard_map/sub | solution.py:164
  279.2 5.8 convert_reduce_fusion.5
  287.0 3.2 multiply_convert_fusion.1
  290.2 11.5 %convert_reduce_fusion.4 = (f32[12,64]{1,0:T(8,128)S(1)}, bf16[12,64,640]{2,1,0:T(8,128)(2,1)S(1)}) fusion(bf16[640,12,64]{0,2,1:T(8,128)(2,1)S(1)} %bitcast.74, f32[12,640,640]{1,2,0:T(8,128)} %get-tuple-element.143, f32[12,640]{1,0:T(8,128)S(1)} %log_add_fusion, pred[640,640]{0,1:T(8,128)(4,1)S(1)} %broadcast_compare_fusion), kind=kOutput, calls=%fused_computation.73 | convolution fusion | flops 645364992 | bytes 22070272 | tf_op jit(solution)/shard_map/hqk,qhd->khd/dot_general | solution.py:184
  302.8 7.9 %convolution_bitcast_fusion = f32[768,2304]{0,1:T(8,128)} fusion(bf16[640,768]{1,0:T(8,128)(2,1)S(1)} %copy-done.29, bf16[640,768]{0,1:T(8,128)(2,1)S(1)} %bitcast.81, bf16[640,768]{0,1:T(8,128)(2,1)S(1)} %bitcast.69, bf16[640,768]{0,1:T(8,128)(2,1)S(1)} %bitcast.65), kind=kOutput, calls=%fused_computation.41 | convolution fusion | flops 2273771520 | bytes 11010048 | tf_op jit(solution)/shard_map/td,tc->dc/dot_general | solution.py:194
  310.7 8.2 %copy.92 = f32[768,2304]{1,0:T(8,128)} copy(f32[768,2304]{0,1:T(8,128)} %convolution_bitcast_fusion) | data formatting | bytes 14155776 | tf_op jit(solution)/shard_map/td,tc->dc/dot_general | solution.py:194
  318.9 6.6 %fusion.75 = f32[768,3072]{1,0:T(8,128)S(1)} fusion(bf16[640,3072]{1,0:T(8,128)(2,1)} %copy-done.9, f32[640,768]{1,0:T(8,128)S(1)} %get-tuple-element.145, f32[768]{0:T(1024)S(1)} %get-tuple-element.111, f32[768]{0:T(1024)S(1)} %get-tuple-element.112, f32[640]{0:T(1024)S(1)} %add_rsqrt_fusion.1, f32[640]{0:T(1024)S(1)} %broadcast_multiply_fusion.7), kind=kOutput, calls=%fused_computation.145 | convolution fusion | flops 3022356480 | bytes 15346688 | tf_op jit(solution)/shard_map/td,tf->df/dot_general | solution.py:139
  325.5 6.0 pad_maximum_fusion
  332.7 40.6 %all-reduce = f32[12,768]{1,0:T(8,128)S(1)} all-reduce(f32[12,768]{1,0:T(8,128)S(1)} %concatenate.15), channel_id=4, replica_groups=mesh['dp'=4,'fsdp'=8] {'dp','fsdp'}, use_global_device_ids=true, to_apply=%region_24.25.clone | all-reduce | flops 9216 | bytes 73728
  374.0 6.1 add_convert_fusion.1
  381.8 194.5 %reduce-scatter.4.cloned.1.call-done = f32[24,5376]{1,0:T(8,128)} async-done(((f32[768,5376]{1,0:T(8,128)}), f32[24,5376]{1,0:T(8,128)}) %reduce-scatter.4.cloned.1.call-update) | async-done | bytes 516112 | tf_op jit(solution)/shard_map/reduce_scatter | solution.py:274
  580.0 13.8 %copy.94 = bf16[1,12,640,640]{3,2,1,0:T(8,128)(2,1)} copy(bf16[1,12,640,640]{2,3,1,0:T(8,128)(2,1)} %bitcast.60) | data formatting | bytes 19660800
  593.8 20.2 %psum.14 = f32[]{:T(128)} all-reduce(f32[]{:T(128)S(6)} %add.237), channel_id=1, replica_groups=mesh['dp'=4,'fsdp'=8] {'fsdp'}, use_global_device_ids=true, to_apply=%region_26.27 | all-reduce | flops 1 | bytes 8 | tf_op jit(solution)/shard_map/psum | solution.py:283
  614.0 13.9 %copy.93 = bf16[1,12,640,640]{3,2,1,0:T(8,128)(2,1)} copy(bf16[1,12,640,640]{2,3,1,0:T(8,128)(2,1)} %get-tuple-element.137) | data formatting | bytes 19660800
  628.0 6.3 psum.15
  (128 shorter events, 28.2 us)
Async XLA Ops:
  7.2 90.8 %all-gather.4.cloned.1.call-start = ((), (), s32[]{:S(2)}) async-start(), calls=%async_computation.2 | async-start | bytes 8515584 | tf_op jit(solution)/shard_map/all_gather | solution.py:256
  9.0 152.9 %all-gather.6.cloned.1.call-start = ((), (), s32[]{:S(2)}) async-start(), calls=%async_computation.3 | async-start | bytes 6082560 | tf_op jit(solution)/shard_map/all_gather | solution.py:257
  10.8 369.3 %reduce-scatter.6.cloned.1.call-start = ((), (), s32[]{:S(2)}) async-start(), calls=%async_computation.5 | async-start | bytes 12165120 | tf_op jit(solution)/shard_map/reduce_scatter | solution.py:275
  83.5 14.0 %copy-start.27 = (s32[1,640]{1,0:T(1,128)S(1)}, s32[1,640]{1,0:T(1,128)}, u32[]{:S(2)}) copy-start(s32[1,640]{1,0:T(1,128)} %param.17) | copy-start | bytes 7684
  83.5 14.4 %copy-start.28 = (bf16[640,768]{1,0:T(8,128)(2,1)S(1)}, bf16[640,768]{1,0:T(8,128)(2,1)}, u32[]{:S(2)}) copy-start(bf16[640,768]{1,0:T(8,128)(2,1)} %param.15) | copy-start | bytes 2949124
  104.5 14.5 %copy-start.4 = (bf16[640,768]{0,1:T(8,128)(2,1)}, bf16[640,768]{0,1:T(8,128)(2,1)S(1)}, u32[]{:S(2)}) copy-start(bf16[640,768]{0,1:T(8,128)(2,1)S(1)} %copy.83) | copy-start | bytes 2949124
  105.2 13.9 %copy-start.2 = (bf16[640,768]{0,1:T(8,128)(2,1)}, bf16[640,768]{0,1:T(8,128)(2,1)S(1)}, u32[]{:S(2)}) copy-start(bf16[640,768]{0,1:T(8,128)(2,1)S(1)} %copy.84) | copy-start | bytes 2949124
  107.1 29.7 %copy-start.16 = (bf16[640,768]{0,1:T(8,128)(2,1)}, bf16[640,768]{0,1:T(8,128)(2,1)S(1)}, u32[]{:S(2)}) copy-start(bf16[640,768]{0,1:T(8,128)(2,1)S(1)} %copy.82) | copy-start | bytes 2949124
  161.9 27.4 %slice-start.2 = ((s8[5898240]{0:T(1024)(128)(4,1)}), s8[4194304]{0:T(1024)(128)(4,1)S(1)}, s32[]{:S(2)}) async-start(s8[5898240]{0:T(1024)(128)(4,1)} %bitcast.79), calls=%async_computation.8 | async-start | bytes 8388608
  165.4 23.9 %slice-start.3 = ((s8[5898240]{0:T(1024)(128)(4,1)}), s8[1703936]{0:T(1024)(128)(4,1)S(1)}, s32[]{:S(2)}) async-start(s8[5898240]{0:T(1024)(128)(4,1)} %bitcast.79), calls=%async_computation.9 | async-start | bytes 3407872
  195.9 17.3 %slice-start = ((s8[8257536]{0:T(1024)(128)(4,1)}), s8[4194304]{0:T(1024)(128)(4,1)S(1)}, s32[]{:S(2)}) async-start(s8[8257536]{0:T(1024)(128)(4,1)} %bitcast.77), calls=%async_computation.6 | async-start | bytes 8388608
  202.3 10.9 %slice-start.1 = ((s8[8257536]{0:T(1024)(128)(4,1)}), s8[4063232]{0:T(1024)(128)(4,1)S(1)}, s32[]{:S(2)}) async-start(s8[8257536]{0:T(1024)(128)(4,1)} %bitcast.77), calls=%async_computation.7 | async-start | bytes 8126464
  231.0 345.2 %reduce-scatter.4.cloned.1.call-start = ((), (), s32[]{:S(2)}) async-start(), calls=%async_computation.4 | async-start | bytes 17031168 | tf_op jit(solution)/shard_map/reduce_scatter | solution.py:274
  250.9 28.3 %copy-start.3 = (bf16[640,768]{0,1:T(8,128)(2,1)S(1)}, bf16[640,768]{0,1:T(8,128)(2,1)}, u32[]{:S(2)}) copy-start(bf16[640,768]{0,1:T(8,128)(2,1)} %copy-done.2) | copy-start | bytes 2949124
  279.2 7.6 %copy-start = (bf16[12,640,640]{1,2,0:T(8,128)(2,1)S(1)}, bf16[12,640,640]{1,2,0:T(8,128)(2,1)}, u32[]{:S(2)}) copy-start(bf16[12,640,640]{1,2,0:T(8,128)(2,1)} %fusion.1) | copy-start | bytes 29491204
  279.2 7.8 %copy-start.5 = (bf16[640,768]{0,1:T(8,128)(2,1)S(1)}, bf16[640,768]{0,1:T(8,128)(2,1)}, u32[]{:S(2)}) copy-start(bf16[640,768]{0,1:T(8,128)(2,1)} %copy-done.4) | copy-start | bytes 2949124
  287.0 14.8 %copy-start.10 = (bf16[12,64,640]{2,1,0:T(8,128)(2,1)}, bf16[12,64,640]{2,1,0:T(8,128)(2,1)S(1)}, u32[]{:S(2)}) copy-start(bf16[12,64,640]{2,1,0:T(8,128)(2,1)S(1)} %get-tuple-element.151) | copy-start | bytes 2949124
  290.2 11.6 %copy-start.17 = (bf16[12,64,640]{2,1,0:T(8,128)(2,1)}, bf16[12,64,640]{2,1,0:T(8,128)(2,1)S(1)}, u32[]{:S(2)}) copy-start(bf16[12,64,640]{2,1,0:T(8,128)(2,1)S(1)} %multiply_convert_fusion.1) | copy-start | bytes 2949124
  290.2 12.5 %copy-start.29 = (bf16[640,768]{1,0:T(8,128)(2,1)S(1)}, bf16[640,768]{1,0:T(8,128)(2,1)}, u32[]{:S(2)}) copy-start(bf16[640,768]{1,0:T(8,128)(2,1)} %param.15) | copy-start | bytes 2949124
  331.5 42.5 %copy-start.7 = (f32[640,768]{1,0:T(8,128)S(1)}, f32[640,768]{1,0:T(8,128)}, u32[]{:S(2)}) copy-start(f32[640,768]{1,0:T(8,128)} %copy-done.6) | copy-start | bytes 5898244
  331.5 42.5 %copy-start.11 = (bf16[12,64,640]{2,1,0:T(8,128)(2,1)S(1)}, bf16[12,64,640]{2,1,0:T(8,128)(2,1)}, u32[]{:S(2)}) copy-start(bf16[12,64,640]{2,1,0:T(8,128)(2,1)} %copy-done.10) | copy-start | bytes 2949124
  373.3 6.8 %copy-start.24 = (f32[12,768]{1,0:T(8,128)}, f32[12,768]{1,0:T(8,128)S(1)}, u32[]{:S(2)}) copy-start(f32[12,768]{1,0:T(8,128)S(1)} %all-reduce) | copy-start | bytes 110596
  614.0 21.0 %copy-start.25 = (f32[12,24]{1,0:T(8,128)S(1)}, f32[12,24]{1,0:T(8,128)}, u32[]{:S(2)}) copy-start(f32[12,24]{1,0:T(8,128)} %param.22) | copy-start | bytes 3460
  614.0 21.0 %copy-start.26 = (f32[12,24]{1,0:T(8,128)S(1)}, f32[12,24]{1,0:T(8,128)}, u32[]{:S(2)}) copy-start(f32[12,24]{1,0:T(8,128)} %param.28) | copy-start | bytes 3460
  614.0 22.5 %copy-start.14 = (f32[120,768]{1,0:T(8,128)S(1)}, f32[120,768]{1,0:T(8,128)}, u32[]{:S(2)}) copy-start(f32[120,768]{1,0:T(8,128)} %param.21) | copy-start | bytes 1105924
  614.0 22.5 %copy-start.15 = (f32[120,768]{1,0:T(8,128)S(1)}, f32[120,768]{1,0:T(8,128)}, u32[]{:S(2)}) copy-start(f32[120,768]{1,0:T(8,128)} %reduce-scatter.6.cloned.1.call-done) | copy-start | bytes 1105924
  614.0 22.5 %copy-start.22 = (f32[120,768]{1,0:T(8,128)S(1)}, f32[120,768]{1,0:T(8,128)}, u32[]{:S(2)}) copy-start(f32[120,768]{1,0:T(8,128)} %param.27) | copy-start | bytes 1105924
  614.0 22.5 %copy-start.23 = (f32[120,768]{1,0:T(8,128)S(1)}, f32[120,768]{1,0:T(8,128)}, u32[]{:S(2)}) copy-start(f32[120,768]{1,0:T(8,128)} %param.24) | copy-start | bytes 1105924
  614.0 23.7 %copy-start.12 = (f32[24,5376]{1,0:T(8,128)S(1)}, f32[24,5376]{1,0:T(8,128)}, u32[]{:S(2)}) copy-start(f32[24,5376]{1,0:T(8,128)} %param.20) | copy-start | bytes 1548292
  614.0 23.7 %copy-start.13 = (f32[24,5376]{1,0:T(8,128)S(1)}, f32[24,5376]{1,0:T(8,128)}, u32[]{:S(2)}) copy-start(f32[24,5376]{1,0:T(8,128)} %reduce-scatter.4.cloned.1.call-done) | copy-start | bytes 1548292
  614.0 23.7 %copy-start.20 = (f32[24,5376]{1,0:T(8,128)S(1)}, f32[24,5376]{1,0:T(8,128)}, u32[]{:S(2)}) copy-start(f32[24,5376]{1,0:T(8,128)} %param.26) | copy-start | bytes 1548292
  614.0 23.7 %copy-start.21 = (f32[24,5376]{1,0:T(8,128)S(1)}, f32[24,5376]{1,0:T(8,128)}, u32[]{:S(2)}) copy-start(f32[24,5376]{1,0:T(8,128)} %param.23) | copy-start | bytes 1548292
  (7 other events, 25.6 us)
Sparse Core Ops, SparseCore 0:
  11.6 80.3 all-gather.3
  95.5 66.3 all-gather.5
  231.2 148.0 reduce-scatter.5
  386.6 189.6 reduce-scatter.3
